TPU v7x, 32 devices: a whole 2x2x4 slice. The times are simulated.
32 devices in a mesh: space: 8 (over z, x), snap: 4 (over y, core).
Axes of the slice: x: 2, y: 2, z: 4, core: 2. Of those that a mesh axis runs over, the one named last changes fastest.
Arguments:
- snapshots: bfloat16 [131072, 512], P('space', 'snap'), may hold values from -6 to 6
- mass_blocks: bfloat16 [1024, 3, 128, 128], P(('space', 'snap')), may hold values from -0.3125 to 0.3125
- neighbours: int32 [1024, 3], P(('space', 'snap')), may hold values from 0 to 1023, as said below
- eigvecs: bfloat16 [512, 128], replicated, may hold values from -0.25 to 0.25
Outputs:
- weighted: bfloat16 [131072, 512], P(('space', 'snap'))
- correlation: float32 [512, 512], P('snap', 'space')
- modes: bfloat16 [131072, 128], P(('space', 'snap'))
Inputs may be any that keep to these rules, and one draw needn't show every extreme that they name: neighbours[b, 0] is b; every entry lies within 4 of b; neighbours[b, 2] lies exactly 4 away from b.
All inputs are finite; a program needn't handle non-finite values.
Results may differ from a plain program's by a relative error of at most 0.0029.
Values may be sent and summed in bfloat16 or wider, within the bound.
A program may use at most 128 MiB of HBM per device.

v0:
```python
import jax
import jax.numpy as jnp
from jax import lax
from jax.sharding import PartitionSpec as P

HB = 4


def shifted(block, axis, distance):
    devices = range(lax.axis_size(axis))
    route = [(i - distance, i) for i in devices if i - distance in devices]
    return lax.ppermute(block, axis, route)


def shards(snapshots, mass_blocks, neighbours, eigvecs):
    local_rows = lax.all_to_all(snapshots, "snap", split_axis=0, concat_axis=1, tiled=True)
    row_count, col_count = local_rows.shape
    block_size = mass_blocks.shape[2]
    rim_rows = HB * block_size
    below_rim = shifted(local_rows[row_count - rim_rows :], ("space", "snap"), 1)
    above_rim = shifted(local_rows[:rim_rows], ("space", "snap"), -1)
    extended = jnp.concatenate([below_rim, local_rows, above_rim], axis=0).reshape(
        -1, block_size, col_count
    )
    first_block = lax.axis_index(("space", "snap")) * (row_count // block_size)
    local_ids = neighbours - first_block + HB
    nearby = extended[local_ids]
    weighted = jnp.einsum("bjrc,bjcs->brs", mass_blocks, nearby, preferred_element_type=jnp.float32)
    weighted = weighted.reshape(row_count, col_count).astype(jnp.bfloat16)
    partial_corr = jnp.dot(weighted.T, local_rows, preferred_element_type=jnp.float32)
    band = lax.psum_scatter(partial_corr, "snap", scatter_dimension=0, tiled=True)
    correlation = lax.psum_scatter(band, "space", scatter_dimension=1, tiled=True)
    cell_total = row_count * lax.axis_size("space") * lax.axis_size("snap")
    correlation = correlation * (1.0 / cell_total)
    modes = jnp.dot(local_rows, eigvecs, preferred_element_type=jnp.float32).astype(jnp.bfloat16)
    return (weighted, correlation, modes)


def solution(mesh):
    in_specs = (
        P("space", "snap"),
        P(("space", "snap"), None, None, None),
        P(("space", "snap"), None),
        P(),
    )
    out_specs = (P(("space", "snap"), None), P("snap", "space"), P(("space", "snap"), None))
    return jax.shard_map(shards, mesh=mesh, in_specs=in_specs, out_specs=out_specs, check_vma=False)
```

profile of v0, /device:TPU:0, one launch (start us, length us, event | category | flops | bytes accessed | tf_op | source)
XLA Modules:
  0.0 218.2 jit_solution(1779734377456381496)
XLA Ops:
  7.2 0.0 copy-start
  7.2 0.0 reduce-scatter.5.cloned.1.call-start
  7.2 52.9 %all_to_all.19 = bf16[4,4096,128]{2,1,0:T(8,128)(2,1)S(1)} all-to-all(bf16[4,4096,128]{2,1,0:T(8,128)(2,1)} %bitcast.30), channel_id=1, replica_groups=mesh['space'=8,'snap'=4] {'snap'}, dimensions={0} | all-to-all | bytes 8388608 | tf_op jit(solution)/shard_map/all_to_all | solution.py:16
  60.1 0.0 copy-start.2
  60.1 0.0 copy-start.5
  60.1 2.0 copy-done.2
  62.1 1.0 fusion
  63.1 2.0 copy.18
  65.2 2.2 %collective-permute-start = (bf16[512,512]{0,1:T(8,128)(2,1)}, bf16[512,512]{0,1:T(8,128)(2,1)}, u32[]{:S(2)}, u32[]{:S(2)}) collective-permute-start(bf16[512,512]{0,1:T(8,128)(2,1)} %bitcast.32), channel_id=1, source_target_pairs={{0,1},{1,2},{2,3},{3,4},{4,5},{5,6},{6,7},{7,8},{8,9},{9,10},{10,1... | collective-permute-start | bytes 1572872 | tf_op jit(solution)/shard_map/ppermute | solution.py:12
  67.4 2.0 copy.20
  69.4 1.3 collective-permute-start.1
  70.7 0.0 copy-done.5
  70.7 0.1 copy.22
  70.8 0.1 reshape.20
  70.9 6.5 %copy.19 = bf16[4096,4,128]{0,2,1:T(8,128)(2,1)} copy(bf16[4096,4,128]{2,0,1:T(8,128)(2,1)} %bitcast.27) | data formatting | bytes 8388608 | tf_op jit(solution)/shard_map/all_to_all | solution.py:16
  77.4 0.0 collective-permute-done
  77.4 0.0 collective-permute-done.1
  77.4 5.8 %pad_maximum_fusion = bf16[5120,512]{0,1:T(8,128)(2,1)} fusion(bf16[512,512]{0,1:T(8,128)(2,1)} %collective-permute-done.1, bf16[4096,512]{0,1:T(8,128)(2,1)} %bitcast.23, bf16[512,512]{0,1:T(8,128)(2,1)} %collective-permute-done), kind=kLoop, calls=%fused_computation.2 | loop fusion | flops 15728640 | bytes 10485760 | tf_op jit(solution)/shard_map/concatenate | solution.py:22
  83.2 7.8 %copy.21 = bf16[5120,512]{1,0:T(8,128)(2,1)} copy(bf16[5120,512]{0,1:T(8,128)(2,1)} %pad_maximum_fusion) | data formatting | bytes 10485760 | tf_op jit(solution)/shard_map/concatenate | solution.py:22
  91.0 9.3 %gather_fusion = bf16[96,128,512]{2,1,0:T(8,128)(2,1)} fusion(bf16[40,128,512]{2,1,0:T(8,128)(2,1)} %bitcast.22, s32[1024]{0:T(1024)S(1)} %pad_clamp_fusion), kind=kCustom, calls=%fused_computation | custom fusion | bytes 25166208 | tf_op jit(solution)/shard_map/gather | solution.py:27
  100.3 0.0 copy-done
  100.3 0.0 copy-start.1
  100.3 7.1 %bitcast_convert_fusion = bf16[32,512,128]{1,2,0:T(8,128)(2,1)S(1)} fusion(bf16[32,3,128,128]{3,2,1,0:T(8,128)(2,1)S(1)} %copy-done, bf16[32,3,128,512]{3,2,1,0:T(8,128)(2,1)} %bitcast.21), kind=kOutput, calls=%fused_computation.1 | convolution fusion | flops 1612709888 | bytes 19922944 | tf_op jit(solution)/shard_map/bjrc,bjcs->brs/dot_general | solution.py:28
  107.4 0.0 copy-start.3
  107.4 2.0 copy-done.3
  109.4 0.0 copy-done.1
  109.4 0.0 copy-start.4
  109.4 3.3 %fusion.1 = f32[512,512]{1,0:T(8,128)} fusion(bf16[4096,512]{1,0:T(8,128)(2,1)S(1)} %bitcast.28, bf16[4096,512]{0,1:T(8,128)(2,1)S(1)} %bitcast.25), kind=kOutput, calls=%fused_computation.8 | convolution fusion | flops 2147483648 | bytes 9437184 | tf_op jit(solution)/shard_map/dot_general | solution.py:30
  112.8 0.0 reduce-scatter.5.cloned.1.call-update
  112.8 0.0 reduce-scatter.7.cloned.1.call-start
  112.8 31.5 %reduce-scatter.5.cloned.1.call-done = f32[128,512]{1,0:T(8,128)} async-done(((f32[512,512]{1,0:T(8,128)}), f32[128,512]{1,0:T(8,128)}) %reduce-scatter.5.cloned.1.call-update) | async-done | bytes 262160 | tf_op jit(solution)/shard_map/reduce_scatter | solution.py:31
  144.3 1.8 copy.25
  146.1 0.0 reduce-scatter.7.cloned.1.call-update
  146.2 0.0 copy-done.4
  146.2 4.5 %convolution_convert_fusion = bf16[4096,128]{1,0:T(8,128)(2,1)} fusion(bf16[4096,512]{0,1:T(8,128)(2,1)} %bitcast.24, bf16[512,128]{1,0:T(8,128)(2,1)S(1)} %copy-done.4), kind=kOutput, calls=%fused_computation.3 | convolution fusion | flops 537395200 | bytes 5373952 | tf_op jit(solution)/shard_map/dot_general | solution.py:35
  150.6 59.2 %reduce-scatter.7.cloned.1.call-done = f32[64,128]{1,0:T(8,128)} async-done(((f32[512,128]{1,0:T(8,128)}), f32[64,128]{1,0:T(8,128)}) %reduce-scatter.7.cloned.1.call-update) | async-done | bytes 32784
  209.8 0.8 copy.26
  210.7 0.7 copy.23
  (3 shorter events, 0.0 us)
Async XLA Ops:
  7.2 93.2 %copy-start = (bf16[32,3,128,128]{3,2,1,0:T(8,128)(2,1)S(1)}, bf16[32,3,128,128]{3,2,1,0:T(8,128)(2,1)}, u32[]{:S(2)}) copy-start(bf16[32,3,128,128]{3,2,1,0:T(8,128)(2,1)} %param.5) | copy-start | bytes 9437188
  7.2 137.2 %reduce-scatter.5.cloned.1.call-start = ((), (), s32[]{:S(2)}) async-start(), calls=%async_computation.3 | async-start | bytes 1310720 | tf_op jit(solution)/shard_map/reduce_scatter | solution.py:31
  60.1 2.0 copy-start.2
  60.1 10.6 %copy-start.5 = (s32[32,3]{0,1:T(4,128)S(1)}, s32[32,3]{0,1:T(4,128)}, u32[]{:S(2)}) copy-start(s32[32,3]{0,1:T(4,128)} %param.6) | copy-start | bytes 1156
  65.2 12.2 %collective-permute-start = (bf16[512,512]{0,1:T(8,128)(2,1)}, bf16[512,512]{0,1:T(8,128)(2,1)}, u32[]{:S(2)}, u32[]{:S(2)}) collective-permute-start(bf16[512,512]{0,1:T(8,128)(2,1)} %bitcast.32), channel_id=1, source_target_pairs={{0,1},{1,2},{2,3},{3,4},{4,5},{5,6},{6,7},{7,8},{8,9},{9,10},{10,1... | collective-permute-start | bytes 1572872 | tf_op jit(solution)/shard_map/ppermute | solution.py:12
  69.4 8.0 %collective-permute-start.1 = (bf16[512,512]{0,1:T(8,128)(2,1)}, bf16[512,512]{0,1:T(8,128)(2,1)}, u32[]{:S(2)}, u32[]{:S(2)}) collective-permute-start(bf16[512,512]{0,1:T(8,128)(2,1)} %bitcast.33), channel_id=1, source_target_pairs={{1,0},{2,1},{3,2},{4,3},{5,4},{6,5},{7,6},{8,7},{9,8},{10,9},{11,1... | collective-permute-start | bytes 1572872 | tf_op jit(solution)/shard_map/ppermute | solution.py:12
  100.3 9.1 %copy-start.1 = (bf16[4096,4,128]{0,2,1:T(8,128)(2,1)S(1)}, bf16[4096,4,128]{0,2,1:T(8,128)(2,1)}, u32[]{:S(2)}) copy-start(bf16[4096,4,128]{0,2,1:T(8,128)(2,1)} %copy.19) | copy-start | bytes 12582916
  107.4 2.0 copy-start.3
  109.4 36.7 %copy-start.4 = (bf16[512,128]{1,0:T(8,128)(2,1)S(1)}, bf16[512,128]{1,0:T(8,128)(2,1)}, u32[]{:S(2)}) copy-start(bf16[512,128]{1,0:T(8,128)(2,1)} %param.7) | copy-start | bytes 393220
  112.8 97.0 %reduce-scatter.7.cloned.1.call-start = ((), (), s32[]{:S(2)}) async-start(), calls=%async_computation.4 | async-start | bytes 294912
Sparse Core Ops, SparseCore 0:
  112.9 31.3 reduce-scatter.4
  147.7 62.0 reduce-scatter.6
where the time goes:
time: 219 us; the launch traced here: 218 us
  waiting for transfers between devices  90.7 us (41%)
  blocking collectives  52.9 us (24%)
  local copies, waits for them, and re-layouts  36.3 us (17%)
  matrix products  14.9 us (7%)
  between operations  14.1 us (6%)
  other arithmetic  5.77 us (3%)
  starting transfers between devices  3.55 us (2%)
    unnamed x3, waiting for transfers between devices  59.2 us
    all_to_all x1, blocking collectives, shards(): lax.all_to_all(snapshots, 'snap', split_axis=0, concat_axis=1, tiled=True)  52.9 us
    reduce_scatter x1, waiting for transfers between devices, shards(): lax.psum_scatter(partial_corr, 'snap', scatter_dimension=0, tiled=True)  31.5 us
    gather x1, local copies, waits for them, and re-layouts, shards(): nearby = extended[local_ids]  9.32 us
    concatenate x1, local copies, waits for them, and re-layouts, shards(): jnp.concatenate([below_rim, local_rows, above_rim], axis=0)  7.83 us
    unnamed x15, local copies, waits for them, and re-layouts  7.36 us
    dot_general x1, matrix products, shards(): jnp.einsum('bjrc,bjcs->brs', mass_blocks, nearby, preferred_element_type=...  7.07 us
    all_to_all x1, local copies, waits for them, and re-layouts, shards(): lax.all_to_all(snapshots, 'snap', split_axis=0, concat_axis=1, tiled=True)  6.46 us
  transfers between devices with their start and end apart: 4, of which 2 were waited for; matrix products, arithmetic and copies ran while one was open for 6% of the time, Pallas kernels for 0%

commit v1 on v0

--- a/solution.py
+++ b/solution.py
@@ -1,9 +1,296 @@
+import functools
+
 import jax
 import jax.numpy as jnp
 from jax import lax
+from jax.experimental import pallas as pl
+from jax.experimental.pallas import tpu as pltpu
 from jax.sharding import PartitionSpec as P
 
 HB = 4
+MESH = pl.DeviceIdType.MESH
+BF16 = jnp.bfloat16
+F32 = jnp.float32
+
+
+def exchange(n, ns, rim, src, ext, bounce, rim_bounce, loc, rim_loc, send_own, recv_own,
+             send_mid, recv_mid, send_main, recv_main, send_fwd, recv_fwd,
+             send_rim, recv_rim, send_out):
+    ny = n // 2
+    s, k = lax.axis_index("space"), lax.axis_index("snap")
+    y, c = k // 2, k % 2
+    partner = 2 * y + 1 - c
+    total = src.shape[0]
+    chip_rows = total // ny
+    rows = chip_rows // 2
+    part = rows - rim
+
+    barrier = pltpu.get_barrier_semaphore()
+    for t in range(1, n):
+        pl.semaphore_signal(barrier, inc=1, device_id=(s, lax.rem(k + t, n)), device_id_type=MESH)
+
+    @pl.when(s > 0)
+    def _():
+        for t in range(n):
+            pl.semaphore_signal(barrier, inc=1, device_id=(s - 1, t), device_id_type=MESH)
+
+    @pl.when(s < ns - 1)
+    def _():
+        for t in range(n):
+            pl.semaphore_signal(barrier, inc=1, device_id=(s + 1, t), device_id_type=MESH)
+
+    load = pltpu.make_async_copy(src.at[pl.ds(y * chip_rows + c * part, rows + rim)], bounce, loc.at[0])
+    load.start()
+    sides = jnp.where(s > 0, 1, 0) + jnp.where(s < ns - 1, 1, 0)
+    pl.semaphore_wait(barrier, n - 1 + n * sides)
+
+    def remote(origin, slab, to_row, count, sends, recvs, device):
+        return pltpu.make_async_remote_copy(
+            src_ref=origin, dst_ref=ext.at[slab, pl.ds(to_row, count)],
+            send_sem=sends, recv_sem=recvs, device_id=device, device_id_type=MESH)
+
+    def rows_of(first, count):
+        return src.at[pl.ds(first, count)]
+
+    mids, mains = [], []
+    for t in range(1, ny):
+        yo = lax.rem(y + t, ny)
+        base = yo * chip_rows
+        for co in range(2):
+            target = (s, 2 * yo + co)
+            mids.append(remote(rows_of(base + part + co * rim, rim), k, rows if co == 0 else rim, rim,
+                               send_mid.at[t, co], recv_mid.at[t, c], target))
+            mains.append(remote(rows_of(base if co == 0 else base + rows + rim, part), k,
+                                rim if co == 0 else 2 * rim, part,
+                                send_main.at[t, co], recv_main.at[t, c], target))
+    own = remote(rows_of(y * chip_rows + (1 - c) * part, rows + rim), k, c * rim, rows + rim,
+                 send_own, recv_own, (s, partner))
+    down = remote(rows_of(0, rim), k, rows + rim, rim, send_out.at[0], recv_rim.at[k], (s - 1, n - 1))
+    up = remote(rows_of(total - rim, rim), k, 0, rim, send_out.at[1], recv_rim.at[k], (s + 1, 0))
+
+    for copy in mids:
+        copy.start()
+    pl.when(s > 0)(down.start)
+    pl.when(s < ns - 1)(up.start)
+    edges = []
+    for target in range(1, n - 1):
+        low = target % 2 == 0
+        first = (target // 2) * chip_rows - rim if low else (target // 2 + 1) * chip_rows
+        edge = remote(rows_of(first, rim), k, 0 if low else rows + rim, rim,
+                      send_rim.at[target], recv_rim.at[k], (s, target))
+        edges.append((target, edge))
+        pl.when(k != target)(edge.start)
+    own.start()
+    for copy in mains:
+        copy.start()
+
+    load.wait()
+    keep = pltpu.make_async_copy(bounce, ext.at[k, pl.ds((1 - c) * rim, rows + rim)], loc.at[1])
+    keep.start()
+    inner = (k > 0) & (k < n - 1)
+    edge_row = jnp.where(c == 0, y * chip_rows - rim, (y + 1) * chip_rows)
+    edge_row = jnp.where(inner, edge_row, 0)
+
+    @pl.when(inner)
+    def _():
+        take = pltpu.make_async_copy(rows_of(edge_row, rim), rim_bounce, rim_loc.at[0])
+        take.start()
+        take.wait()
+        put = pltpu.make_async_copy(rim_bounce, ext.at[k, pl.ds(c * (rows + rim), rim)], rim_loc.at[1])
+        put.start()
+        put.wait()
+
+    forwards = []
+    for t in range(1, ny):
+        yo = lax.rem(y + ny - t, ny)
+        for co in range(2):
+            slab = 2 * yo + co
+            at = (1 - c) * rows + c * rim
+            held = ext.at[slab, pl.ds(at, rim)]
+            remote(held, slab, at, rim, send_mid.at[t, co], recv_mid.at[t, co], (s, partner)).wait_recv()
+            forward = remote(held, slab, c * (rows + rim), rim,
+                             send_fwd.at[t, co], recv_fwd.at[t, co], (s, partner))
+            forward.start()
+            forwards.append((slab, t, co, forward))
+
+    own_slab = partner
+    remote(ext.at[own_slab, pl.ds(0, rows + rim)], own_slab, (1 - c) * rim, rows + rim,
+           send_own, recv_own, (s, partner)).wait_recv()
+    lowest = (k == 0) & (s == 0)
+    highest = (k == n - 1) & (s == ns - 1)
+    for slab in range(n):
+        rim_at = ext.at[slab, pl.ds(c * (rows + rim), rim)]
+        expected = jnp.logical_not(lowest | highest | (inner & (k == slab)))
+
+        @pl.when(expected)
+        def _(rim_at=rim_at, slab=slab):
+            remote(rim_at, slab, c * (rows + rim), rim, send_rim.at[0], recv_rim.at[slab],
+                   (s, partner)).wait_recv()
+    for slab, t, co, forward in forwards:
+        to = (1 - c) * (rows + rim)
+        remote(ext.at[slab, pl.ds(to, rim)], slab, to, rim, send_fwd.at[t, co], recv_fwd.at[t, co],
+               (s, partner)).wait_recv()
+        at = rim + c * rim
+        remote(ext.at[slab, pl.ds(at, part)], slab, at, part, send_main.at[t, co], recv_main.at[t, co],
+               (s, partner)).wait_recv()
+
+    keep.wait()
+    for copy in mids + mains + [own] + [entry[3] for entry in forwards]:
+        copy.wait_send()
+    pl.when(s > 0)(down.wait_send)
+    pl.when(s < ns - 1)(up.wait_send)
+    for target, edge in edges:
+        pl.when(k != target)(edge.wait_send)
+
+
+def compute(n, per_step, near, ext, mass, eig, weighted, modes, corr):
+    step = pl.program_id(0)
+    size = mass.shape[2]
+
+    @pl.when(step == 0)
+    def _():
+        corr[...] = jnp.zeros_like(corr)
+
+    def block_at(index):
+        first = pl.multiple_of(index * size, size)
+        return jnp.concatenate([ext[slab, pl.ds(first, size), :] for slab in range(n)], axis=1)
+
+    for local in range(per_step):
+        row = step * per_step + local
+        masses = jnp.concatenate([mass[local, j] for j in range(mass.shape[1])], axis=1)
+        fields = jnp.concatenate([block_at(near[row, j]) for j in range(mass.shape[1])], axis=0)
+        product = jnp.dot(masses, fields, preferred_element_type=F32)
+        weighted[pl.ds(local * size, size), :] = product.astype(BF16)
+    first = pl.multiple_of((step * per_step + HB) * size, size)
+    here = jnp.concatenate([ext[slab, pl.ds(first, per_step * size), :] for slab in range(n)], axis=1)
+    modes[...] = jnp.dot(here, eig[...], preferred_element_type=F32).astype(BF16)
+    sums = lax.dot_general(here, weighted[...], (((0,), (0,)), ((), ())), preferred_element_type=F32)
+    width = corr.shape[2]
+    for band in range(n):
+        corr[band] += sums[:, band * width:(band + 1) * width]
+
+
+def reduce_kernel(n, ns, scale, part, out, recv1, send2, recv2, send3, recv3, send4, recv4,
+                  s1, r1, s2, r2, s3, r3, s4, r4):
+    ny, nz = n // 2, ns // 2
+    s, k = lax.axis_index("space"), lax.axis_index("snap")
+    y, c, z, x = k // 2, k % 2, s // 2, s % 2
+    xo = 1 - x
+    barrier = pltpu.get_barrier_semaphore()
+    peers = [(s, 2 * y + 1 - c), (2 * z + xo, k)]
+    peers += [(s, 2 * lax.rem(y + t, ny) + c) for t in range(1, ny)]
+    peers += [(2 * lax.rem(z + t, nz) + x, k) for t in range(1, nz)]
+    for peer in peers:
+        pl.semaphore_signal(barrier, inc=1, device_id=peer, device_id_type=MESH)
+    pl.semaphore_wait(barrier, len(peers))
+
+    def remote(origin, target, sends, recvs, device):
+        copy = pltpu.make_async_remote_copy(src_ref=origin, dst_ref=target, send_sem=sends,
+                                            recv_sem=recvs, device_id=device, device_id_type=MESH)
+        copy.start()
+        return copy
+
+    order = [lax.rem(y + t, ny) for t in range(1, ny)] + [y]
+    first = [[remote(part.at[2 * yo + 1 - c, :, half], recv1.at[i, h], s1.at[i, h], r1.at[i, h],
+                     (s, 2 * y + 1 - c)) for h, half in enumerate((xo, x))] for i, yo in enumerate(order)]
+    second = []
+    for i, yo in enumerate(order[:-1]):
+        for h, half in enumerate((xo, x)):
+            first[i][h].wait()
+            send2[i, h] = part[2 * yo + c, :, half] + recv1[i, h]
+            second.append((i, h, remote(send2.at[i, h], recv2.at[i, h], s2.at[i, h], r2.at[i, h],
+                                        (s, 2 * yo + c))))
+
+    def gathered(h, half):
+        first[ny - 1][h].wait()
+        value = part[2 * y + c, :, half] + recv1[ny - 1, h]
+        for i, g, copy in second:
+            if g == h:
+                copy.wait()
+                value = value + recv2[i, h]
+        return value
+
+    send3[...] = gathered(0, xo)
+    third = remote(send3, recv3, s3, r3, (2 * z + xo, k))
+    kept = gathered(1, x)
+    third.wait()
+    send4[...] = kept + recv3[...]
+    last = []
+    for t in range(1, nz):
+        zo = lax.rem(z + t, nz)
+        last.append(remote(send4.at[zo], recv4.at[t - 1], s4.at[t - 1], r4.at[t - 1], (2 * zo + x, k)))
+    value = send4[z]
+    for i, copy in enumerate(last):
+        copy.wait()
+        value = value + recv4[i]
+    out[...] = value * scale
+
+
+def fast_shards(n, ns, snapshots, mass_blocks, neighbours, eigvecs):
+    block_rows, picks, size, _ = mass_blocks.shape
+    total, width = snapshots.shape
+    rim = HB * size
+    rows = total // n
+    snaps = n * width
+    sem = pltpu.SemaphoreType.DMA
+    ny, nz = n // 2, ns // 2
+    ext = pl.pallas_call(
+        functools.partial(exchange, n, ns, rim),
+        out_shape=jax.ShapeDtypeStruct((n, rows + 2 * rim, width), BF16),
+        in_specs=[pl.BlockSpec(memory_space=pl.ANY)],
+        out_specs=pl.BlockSpec(memory_space=pl.ANY),
+        scratch_shapes=[
+            pltpu.VMEM((rows + rim, width), BF16), pltpu.VMEM((rim, width), BF16),
+            sem((2,)), sem((2,)), sem, sem,
+            sem((ny, 2)), sem((ny, 2)), sem((ny, 2)), sem((ny, 2)), sem((ny, 2)), sem((ny, 2)),
+            sem((n,)), sem((n,)), sem((2,)),
+        ],
+        compiler_params=pltpu.CompilerParams(collective_id=0, has_side_effects=True),
+        name="exchange",
+    )(snapshots)
+    first_block = (lax.axis_index("space") * n + lax.axis_index("snap")) * block_rows
+    near = neighbours - first_block + HB
+    per_step = 4 if block_rows % 4 == 0 else 1
+    modes_count = eigvecs.shape[1]
+    weighted, modes, corr = pl.pallas_call(
+        functools.partial(compute, n, per_step),
+        out_shape=(jax.ShapeDtypeStruct((rows, snaps), BF16),
+                   jax.ShapeDtypeStruct((rows, modes_count), BF16),
+                   jax.ShapeDtypeStruct((n, snaps, width), F32)),
+        grid_spec=pltpu.PrefetchScalarGridSpec(
+            num_scalar_prefetch=1,
+            grid=(block_rows // per_step,),
+            in_specs=[
+                pl.BlockSpec(ext.shape, lambda i, near: (0, 0, 0)),
+                pl.BlockSpec((per_step, picks, size, size), lambda i, near: (i, 0, 0, 0)),
+                pl.BlockSpec(eigvecs.shape, lambda i, near: (0, 0)),
+            ],
+            out_specs=[
+                pl.BlockSpec((per_step * size, snaps), lambda i, near: (i, 0)),
+                pl.BlockSpec((per_step * size, modes_count), lambda i, near: (i, 0)),
+                pl.BlockSpec((n, snaps, width), lambda i, near: (0, 0, 0)),
+            ],
+        ),
+        compiler_params=pltpu.CompilerParams(vmem_limit_bytes=48 * 2**20),
+        name="weigh",
+    )(near, ext, mass_blocks, eigvecs)
+    tile = snaps // ns
+    piece = (nz, tile, width)
+    vmem = pltpu.VMEM
+    out = pl.pallas_call(
+        functools.partial(reduce_kernel, n, ns, 1.0 / (total * ns)),
+        out_shape=jax.ShapeDtypeStruct((tile, width), F32),
+        in_specs=[pl.BlockSpec(memory_space=pltpu.VMEM)],
+        out_specs=pl.BlockSpec(memory_space=pltpu.VMEM),
+        scratch_shapes=[
+            vmem((ny, 2) + piece, F32), vmem((ny, 2) + piece, F32), vmem((ny, 2) + piece, F32),
+            vmem(piece, F32), vmem(piece, F32), vmem(piece, F32), vmem(piece, F32),
+            sem((ny, 2)), sem((ny, 2)), sem((ny, 2)), sem((ny, 2)), sem, sem, sem((nz,)), sem((nz,)),
+        ],
+        compiler_params=pltpu.CompilerParams(collective_id=1, has_side_effects=True),
+        name="reduce",
+    )(corr.reshape(n, nz, 2, tile, width))
+    return weighted, out.T, modes
 
 
 def shifted(block, axis, distance):
@@ -12,7 +299,7 @@
     return lax.ppermute(block, axis, route)
 
 
-def shards(snapshots, mass_blocks, neighbours, eigvecs):
+def plain_shards(snapshots, mass_blocks, neighbours, eigvecs):
     local_rows = lax.all_to_all(snapshots, "snap", split_axis=0, concat_axis=1, tiled=True)
     row_count, col_count = local_rows.shape
     block_size = mass_blocks.shape[2]
@@ -37,6 +324,17 @@
 
 
 def solution(mesh):
+    n, ns = mesh.shape["snap"], mesh.shape["space"]
+
+    def shards(snapshots, mass_blocks, neighbours, eigvecs):
+        width = snapshots.shape[1]
+        rows = snapshots.shape[0] // n
+        tile = n * width // ns
+        whole = width % 128 == 0 and tile % 8 == 0 and n % 2 == 0 and ns % 2 == 0
+        if whole and n > 2 and ns > 2 and rows > 2 * HB * mass_blocks.shape[2]:
+            return fast_shards(n, ns, snapshots, mass_blocks, neighbours, eigvecs)
+        return plain_shards(snapshots, mass_blocks, neighbours, eigvecs)
+
     in_specs = (
         P("space", "snap"),
         P(("space", "snap"), None, None, None),

time: 219 us -> 90.4 us (0.41)
  waiting for transfers between devices: 90.7 us -> 0 us
  Pallas kernels: 0 us -> 86.3 us
  blocking collectives: 52.9 us -> 0 us
  local copies, waits for them, and re-layouts: 36.3 us -> 2.44 us
  matrix products: 14.9 us -> 0 us
  between operations: 14.1 us -> 0.68 us
  other arithmetic: 5.77 us -> 0.69 us
  starting transfers between devices: 3.55 us -> 0 us
    pallas_call x0 -> x3, Pallas kernels: none -> 86.3 us  [the longest x1 55.7 us: fast_shards(): pl.pallas_call(functools.partial(exchange, n, ns, rim), out_shape=jax.Sha...]
    unnamed x3 -> x0, waiting for transfers between devices: 59.2 us -> none
    all_to_all x1 -> x0, blocking collectives: 52.9 us -> none  [shards(): lax.all_to_all(snapshots, 'snap', split_axis=0, concat_axis=1, tiled=True)]
    reduce_scatter x1 -> x0, waiting for transfers between devices: 31.5 us -> none  [shards(): lax.psum_scatter(partial_corr, 'snap', scatter_dimension=0, tiled=True)]
    dot_general x3 -> x0, matrix products: 14.9 us -> none  [the longest x1 7.07 us: shards(): jnp.einsum('bjrc,bjcs->brs', mass_blocks, nearby, preferred_element_type=...]
    gather x1 -> x0, local copies, waits for them, and re-layouts: 9.32 us -> none  [shards(): nearby = extended[local_ids]]
    concatenate x1 -> x0, local copies, waits for them, and re-layouts: 7.83 us -> none  [shards(): jnp.concatenate([below_rim, local_rows, above_rim], axis=0)]
    all_to_all x1 -> x0, local copies, waits for them, and re-layouts: 6.46 us -> none  [shards(): lax.all_to_all(snapshots, 'snap', split_axis=0, concat_axis=1, tiled=True)]
  transfers between devices with their start and end apart: 4 -> 0, of which waited for: 2 -> 0; matrix products, arithmetic and copies ran while one was open for 6% -> 0% of each run, Pallas kernels for 0% -> 0%
where the time goes in v1:
time: 90.4 us; the launch traced here: 90.1 us
  Pallas kernels  86.3 us (95%)
  local copies, waits for them, and re-layouts  2.44 us (3%)
    pallas_call x1, Pallas kernels, fast_shards(): pl.pallas_call(functools.partial(exchange, n, ns, rim), out_shape=jax.Sha...  55.7 us
    pallas_call x1, Pallas kernels, fast_shards(): pl.pallas_call(functools.partial(reduce_kernel, n, ns, 1.0 / (total * ns)...  19.8 us
    pallas_call x1, Pallas kernels, fast_shards(): pl.pallas_call(functools.partial(compute, n, per_step), out_shape=(jax.Sh...  10.8 us
    unnamed x7, local copies, waits for them, and re-layouts  2.35 us

profile of v1, /device:TPU:0, one launch (start us, length us, event | category | flops | bytes accessed | tf_op | source)
XLA Modules:
  0.0 90.1 jit_solution(14392679558550031710)
XLA Ops:
  0.6 0.7 broadcast_subtract_fusion
  1.3 0.1 copy.9
  1.4 0.0 copy-start
  1.4 0.0 copy-start.2
  1.4 55.7 %exchange.1.ext = bf16[4,5120,128]{2,1,0:T(8,128)(2,1)} custom-call(bf16[16384,128]{1,0:T(8,128)(2,1)} %src.1), custom_call_target="tpu_custom_call" | custom-call | tf_op jit(solution)/shard_map/exchange/pallas_call | solution.py:237
  57.2 0.0 copy-done
  57.2 0.0 copy-done.2
  57.2 10.8 %weigh.1 = (bf16[4096,512]{1,0:T(8,128)(2,1)}, bf16[4096,128]{1,0:T(8,128)(2,1)}, f32[4,512,128]{2,1,0:T(8,128)S(1)}) custom-call(s32[32,3]{1,0:T(8,128)S(1)} %broadcast_add_fusion.near, bf16[4,5120,128]{2,1,0:T(8,128)(2,1)} %exchange.1.ext, bf16[32,3,128,128]{3,2,1,0:T(8,128)(2,1)S(1)} %copy-done, bf16[512,128]{1,0:T(8,128)(2,1)S(1)} %copy-done.2), custom_call_target="tpu_custom_call" | custom-call | tf_op jit(solution)/shard_map/weigh/pallas_call | solution.py:255
  68.0 0.0 copy-start.1
  68.0 1.0 %copy-done.1 = f32[4,512,128]{2,1,0:T(8,128)} copy-done((f32[4,512,128]{2,1,0:T(8,128)}, f32[4,512,128]{2,1,0:T(8,128)S(1)}, u32[]{:S(2)}) %copy-start.1) | copy-done | bytes 1048600
  69.0 19.8 %reduce.1 = f32[64,128]{1,0:T(8,128)} custom-call(f32[4,4,2,64,128]{4,3,2,1,0:T(8,128)} %bitcast.2), custom_call_target="tpu_custom_call" | custom-call | tf_op jit(solution)/shard_map/reduce/pallas_call | solution.py:280
  88.8 1.4 %copy.13 = f32[128,64]{0,1:T(8,128)} copy(f32[128,64]{0,1:T(8,128)} %bitcast.3) | data formatting | bytes 65536
  (1 shorter events, 0.0 us)
Async XLA Ops:
  1.4 55.8 %copy-start = (bf16[32,3,128,128]{3,2,1,0:T(8,128)(2,1)S(1)}, bf16[32,3,128,128]{3,2,1,0:T(8,128)(2,1)}, u32[]{:S(2)}) copy-start(bf16[32,3,128,128]{3,2,1,0:T(8,128)(2,1)} %mass.1) | copy-start | bytes 9437188
  1.4 55.8 %copy-start.2 = (bf16[512,128]{1,0:T(8,128)(2,1)S(1)}, bf16[512,128]{1,0:T(8,128)(2,1)}, u32[]{:S(2)}) copy-start(bf16[512,128]{1,0:T(8,128)(2,1)} %eig.1) | copy-start | bytes 393220
  68.0 1.0 %copy-start.1 = (f32[4,512,128]{2,1,0:T(8,128)}, f32[4,512,128]{2,1,0:T(8,128)S(1)}, u32[]{:S(2)}) copy-start(f32[4,512,128]{2,1,0:T(8,128)S(1)} %get-tuple-element.7) | copy-start | bytes 3145732

commit v2 on v0

--- a/solution.py
+++ b/solution.py
@@ -1,9 +1,294 @@
+import functools
+
 import jax
 import jax.numpy as jnp
 from jax import lax
+from jax.experimental import pallas as pl
+from jax.experimental.pallas import tpu as pltpu
 from jax.sharding import PartitionSpec as P
 
 HB = 4
+MESH = pl.DeviceIdType.MESH
+BF16 = jnp.bfloat16
+F32 = jnp.float32
+
+
+def reduce_tiles(n, ns, part, recv1, send2, recv2, send3, recv3, send4, recv4,
+                 s1, r1, s2, r2, s3, r3, s4, r4):
+    ny, nz = n // 2, ns // 2
+    s, k = lax.axis_index("space"), lax.axis_index("snap")
+    y, c, z, x = k // 2, k % 2, s // 2, s % 2
+    xo = 1 - x
+
+    def remote(origin, target, sends, recvs, device):
+        copy = pltpu.make_async_remote_copy(src_ref=origin, dst_ref=target, send_sem=sends,
+                                            recv_sem=recvs, device_id=device, device_id_type=MESH)
+        copy.start()
+        return copy
+
+    order = [lax.rem(y + t, ny) for t in range(1, ny)] + [y]
+    first = [[remote(part.at[2 * yo + 1 - c, :, half], recv1.at[i, h], s1.at[i, h], r1.at[i, h],
+                     (s, 2 * y + 1 - c)) for h, half in enumerate((xo, x))] for i, yo in enumerate(order)]
+    second = []
+    for i, yo in enumerate(order[:-1]):
+        for h, half in enumerate((xo, x)):
+            first[i][h].wait()
+            send2[i, h] = part[2 * yo + c, :, half] + recv1[i, h]
+            second.append((i, h, remote(send2.at[i, h], recv2.at[i, h], s2.at[i, h], r2.at[i, h],
+                                        (s, 2 * yo + c))))
+
+    def gathered(h, half):
+        first[ny - 1][h].wait()
+        value = part[2 * y + c, :, half] + recv1[ny - 1, h]
+        for i, g, copy in second:
+            if g == h:
+                copy.wait()
+                value = value + recv2[i, h]
+        return value
+
+    send3[...] = gathered(0, xo)
+    third = remote(send3, recv3, s3, r3, (2 * z + xo, k))
+    kept = gathered(1, x)
+    third.wait()
+    send4[...] = kept + recv3[...]
+    last = []
+    for t in range(1, nz):
+        zo = lax.rem(z + t, nz)
+        last.append(remote(send4.at[zo], recv4.at[t - 1], s4.at[t - 1], r4.at[t - 1], (2 * zo + x, k)))
+    value = send4[z]
+    for i, copy in enumerate(last):
+        copy.wait()
+        value = value + recv4[i]
+    return value
+
+
+def fused(n, ns, size, scale, near, src, mass_hbm, eig, weighted_hbm, modes_hbm, corr_out,
+          ext, win, mass, weighted, modes, part, loc, own_sems, out_sems,
+          send_mid, recv_mid, send_main, recv_main, send_fwd, recv_fwd,
+          send_rim, recv_rim, send_out, *reduce_refs):
+    ny, nz = n // 2, ns // 2
+    s, k = lax.axis_index("space"), lax.axis_index("snap")
+    y, c, z, x = k // 2, k % 2, s // 2, s % 2
+    partner = 2 * y + 1 - c
+    rim = HB * size
+    total = src.shape[0]
+    chip_rows = total // ny
+    rows = chip_rows // 2
+    pieces = rows // rim
+    width = src.shape[1]
+
+    barrier = pltpu.get_barrier_semaphore()
+    for t in range(1, n):
+        pl.semaphore_signal(barrier, inc=1, device_id=(s, lax.rem(k + t, n)), device_id_type=MESH)
+    for t in range(1, nz):
+        pl.semaphore_signal(barrier, inc=1, device_id=(2 * lax.rem(z + t, nz) + x, k), device_id_type=MESH)
+
+    @pl.when(s > 0)
+    def _():
+        for t in range(n):
+            pl.semaphore_signal(barrier, inc=1, device_id=(s - 1, t), device_id_type=MESH)
+
+    @pl.when(s < ns - 1)
+    def _():
+        for t in range(n):
+            pl.semaphore_signal(barrier, inc=1, device_id=(s + 1, t), device_id_type=MESH)
+
+    def rows_of(first, count):
+        return src.at[pl.ds(first, count)]
+
+    keep = pltpu.make_async_copy(rows_of(y * chip_rows + c * (rows - rim), rows + rim),
+                                 ext.at[k, pl.ds((1 - c) * rim, rows + rim)], loc.at[0])
+    keep.start()
+    inner = (k > 0) & (k < n - 1)
+    edge_row = jnp.where(inner, jnp.where(c == 0, y * chip_rows - rim, (y + 1) * chip_rows), 0)
+    edge_keep = pltpu.make_async_copy(rows_of(edge_row, rim), ext.at[k, pl.ds(c * (rows + rim), rim)],
+                                      loc.at[1])
+    pl.when(inner)(edge_keep.start)
+    fetch = pltpu.make_async_copy(mass_hbm, mass, loc.at[2])
+    fetch.start()
+    part[...] = jnp.zeros_like(part)
+
+    sides = jnp.where(s > 0, 1, 0) + jnp.where(s < ns - 1, 1, 0)
+    pl.semaphore_wait(barrier, n - 1 + nz - 1 + n * sides)
+
+    def remote(origin, slab, to_row, count, sends, recvs, device):
+        return pltpu.make_async_remote_copy(
+            src_ref=origin, dst_ref=ext.at[slab, pl.ds(to_row, count)],
+            send_sem=sends, recv_sem=recvs, device_id=device, device_id_type=MESH)
+
+    mids, mains = [], []
+    for t in range(1, ny):
+        yo = lax.rem(y + t, ny)
+        base = yo * chip_rows
+        for co in range(2):
+            mids.append(remote(rows_of(base + rows - rim + co * rim, rim), k, rows if co == 0 else rim, rim,
+                               send_mid.at[t, co], recv_mid.at[t, c], (s, 2 * yo + co)))
+    for p in range(pieces - 1):
+        for t in range(1, ny):
+            yo = lax.rem(y + t, ny)
+            base = yo * chip_rows
+            for co in range(2):
+                first = (pieces - 2 - p) * rim if co == 0 else rows + (1 + p) * rim
+                to = (pieces - 1 - p) * rim if co == 0 else (2 + p) * rim
+                mains.append(remote(rows_of(base + first, rim), k, to, rim, send_main.at[t, co, p],
+                                    recv_main.at[t, c, p], (s, 2 * yo + co)))
+    own = remote(rows_of(y * chip_rows + (1 - c) * (rows - rim), rows + rim), k, c * rim, rows + rim,
+                 own_sems.at[0], own_sems.at[1], (s, partner))
+    down = remote(rows_of(0, rim), k, rows + rim, rim, send_out.at[0], recv_rim.at[k], (s - 1, n - 1))
+    up = remote(rows_of(total - rim, rim), k, 0, rim, send_out.at[1], recv_rim.at[k], (s + 1, 0))
+
+    for copy in mids:
+        copy.start()
+    own.start()
+    pl.when(s > 0)(down.start)
+    pl.when(s < ns - 1)(up.start)
+    edges = []
+    for target in range(1, n - 1):
+        low = target % 2 == 0
+        first = (target // 2) * chip_rows - rim if low else (target // 2 + 1) * chip_rows
+        edge = remote(rows_of(first, rim), k, 0 if low else rows + rim, rim,
+                      send_rim.at[target], recv_rim.at[k], (s, target))
+        edges.append((target, edge))
+        pl.when(k != target)(edge.start)
+    for copy in mains:
+        copy.start()
+
+    def wait_for(slab, to_row, count, recvs):
+        remote(ext.at[slab, pl.ds(to_row, count)], slab, to_row, count, own_sems.at[0], recvs,
+               (s, partner)).wait_recv()
+
+    forwards = []
+    at, to = (1 - c) * rows + c * rim, (1 - c) * (rows + rim)
+    for t in range(1, ny):
+        for co in range(2):
+            slab = 2 * lax.rem(y + ny - t, ny) + co
+            wait_for(slab, at, rim, recv_mid.at[t, co])
+            forward = remote(ext.at[slab, pl.ds(at, rim)], slab, c * (rows + rim), rim,
+                             send_fwd.at[t, co], recv_fwd.at[t, co], (s, partner))
+            forward.start()
+            forwards.append((slab, t, co, forward))
+    keep.wait()
+    wait_for(partner, (1 - c) * rim, rows + rim, own_sems.at[1])
+    for slab, t, co, forward in forwards:
+        wait_for(slab, to, rim, recv_fwd.at[t, co])
+    fetch.wait()
+
+    def slot_of(order):
+        return jnp.where(c == 1, order, pieces + 1 - order)
+
+    def admit(order):
+        slot = slot_of(order)
+        place = lax.rem(slot, 3) * HB
+        for slab in range(n):
+            held = ext[slab, pl.ds(pl.multiple_of(slot * rim, rim), rim), :]
+            win[pl.ds(place, HB), :, slab * width:(slab + 1) * width] = held.reshape(HB, size, width)
+
+    def out_copies(group):
+        first = pl.multiple_of((slot_of(group + 1) - 1) * rim, rim)
+        return [pltpu.make_async_copy(held.at[pl.ds(first, rim)], target.at[pl.ds(first, rim)],
+                                      out_sems.at[i, group])
+                for i, (held, target) in enumerate(((weighted, weighted_hbm), (modes, modes_hbm)))]
+
+    def work(group):
+        slot = slot_of(group + 1)
+        first = pl.multiple_of((slot - 1) * rim, rim)
+        for i in range(HB):
+            row = (slot - 1) * HB + i
+            masses = jnp.concatenate([mass[row, j] for j in range(mass.shape[1])], axis=1)
+            fields = jnp.concatenate(
+                [win[near[row, j]] for j in range(mass.shape[1])], axis=0)
+            product = jnp.dot(masses, fields, preferred_element_type=F32)
+            weighted[pl.ds(pl.multiple_of(first + i * size, size), size), :] = product.astype(BF16)
+        here = win[pl.ds(lax.rem(slot, 3) * HB, HB)].reshape(rim, n * width)
+        modes[pl.ds(first, rim), :] = jnp.dot(here, eig[...], preferred_element_type=F32).astype(BF16)
+        sums = lax.dot_general(here, weighted[pl.ds(first, rim), :], (((0,), (0,)), ((), ())),
+                               preferred_element_type=F32)
+        tile = part.shape[3]
+        for band in range(n):
+            for index in range(ns):
+                part[band, index // 2, index % 2] += sums[index * tile:(index + 1) * tile,
+                                                          band * width:(band + 1) * width]
+        for copy in out_copies(group):
+            copy.start()
+
+    admit(0)
+    admit(1)
+
+    @pl.loop(0, pieces - 1)
+    def _(p):
+        place = pl.multiple_of(slot_of(p + 2) * rim, rim)
+        for slab, t, co, forward in forwards:
+            wait_for(slab, place, rim, recv_main.at[t, co, p])
+        admit(p + 2)
+        work(p)
+
+    lowest = (k == 0) & (s == 0)
+    highest = (k == n - 1) & (s == ns - 1)
+    pl.when(inner)(edge_keep.wait)
+    for slab in range(n):
+        expected = jnp.logical_not(lowest | highest | (inner & (k == slab)))
+
+        @pl.when(expected)
+        def _(slab=slab):
+            wait_for(slab, c * (rows + rim), rim, recv_rim.at[slab])
+    admit(pieces + 1)
+    work(pieces - 1)
+
+    corr_out[...] = reduce_tiles(n, ns, part, *reduce_refs) * scale
+
+    for copy in mids + mains + [own] + [entry[3] for entry in forwards]:
+        copy.wait_send()
+    pl.when(s > 0)(down.wait_send)
+    pl.when(s < ns - 1)(up.wait_send)
+    for target, edge in edges:
+        pl.when(k != target)(edge.wait_send)
+
+    @pl.loop(0, pieces)
+    def _(group):
+        for copy in out_copies(group):
+            copy.wait()
+
+
+def fast_shards(n, ns, snapshots, mass_blocks, neighbours, eigvecs):
+    block_rows, picks, size, _ = mass_blocks.shape
+    total, width = snapshots.shape
+    rim = HB * size
+    rows = total // n
+    snaps = n * width
+    pieces = rows // rim
+    sem = pltpu.SemaphoreType.DMA
+    vmem = pltpu.VMEM
+    ny, nz = n // 2, ns // 2
+    tile = snaps // ns
+    piece = (nz, tile, width)
+    first_block = (lax.axis_index("space") * n + lax.axis_index("snap")) * block_rows
+    near = lax.rem(neighbours - first_block + HB, 3 * HB)
+    modes_count = eigvecs.shape[1]
+    anywhere = pl.BlockSpec(memory_space=pl.ANY)
+    weighted, modes, corr = pl.pallas_call(
+        functools.partial(fused, n, ns, size, 1.0 / (total * ns)),
+        out_shape=(jax.ShapeDtypeStruct((rows, snaps), BF16),
+                   jax.ShapeDtypeStruct((rows, modes_count), BF16),
+                   jax.ShapeDtypeStruct((tile, width), F32)),
+        in_specs=[pl.BlockSpec(memory_space=pltpu.SMEM), anywhere, anywhere,
+                  pl.BlockSpec(memory_space=pltpu.VMEM)],
+        out_specs=(anywhere, anywhere, pl.BlockSpec(memory_space=pltpu.VMEM)),
+        scratch_shapes=[
+            vmem((n, rows + 2 * rim, width), BF16), vmem((3 * HB, size, snaps), BF16),
+            vmem(mass_blocks.shape, BF16), vmem((rows, snaps), BF16), vmem((rows, modes_count), BF16),
+            vmem((n, nz, 2, tile, width), F32),
+            sem((3,)), sem((2,)), sem((2, pieces)),
+            sem((ny, 2)), sem((ny, 2)), sem((ny, 2, pieces - 1)), sem((ny, 2, pieces - 1)),
+            sem((ny, 2)), sem((ny, 2)), sem((n,)), sem((n,)), sem((2,)),
+            vmem((ny, 2) + piece, F32), vmem((ny, 2) + piece, F32), vmem((ny, 2) + piece, F32),
+            vmem(piece, F32), vmem(piece, F32), vmem(piece, F32), vmem(piece, F32),
+            sem((ny, 2)), sem((ny, 2)), sem((ny, 2)), sem((ny, 2)), sem, sem, sem((nz,)), sem((nz,)),
+        ],
+        compiler_params=pltpu.CompilerParams(collective_id=0, has_side_effects=True,
+                                             vmem_limit_bytes=62 * 2**20),
+        name="fused",
+    )(near, snapshots, mass_blocks, eigvecs)
+    return weighted, corr.T, modes
 
 
 def shifted(block, axis, distance):
@@ -12,7 +297,7 @@
     return lax.ppermute(block, axis, route)
 
 
-def shards(snapshots, mass_blocks, neighbours, eigvecs):
+def plain_shards(snapshots, mass_blocks, neighbours, eigvecs):
     local_rows = lax.all_to_all(snapshots, "snap", split_axis=0, concat_axis=1, tiled=True)
     row_count, col_count = local_rows.shape
     block_size = mass_blocks.shape[2]
@@ -37,6 +322,18 @@
 
 
 def solution(mesh):
+    n, ns = mesh.shape["snap"], mesh.shape["space"]
+
+    def shards(snapshots, mass_blocks, neighbours, eigvecs):
+        width = snapshots.shape[1]
+        rows = snapshots.shape[0] // n
+        tile = n * width // ns
+        rim = HB * mass_blocks.shape[2]
+        whole = width % 128 == 0 and tile % 8 == 0 and n % 2 == 0 and ns % 2 == 0
+        if whole and n > 2 and ns > 2 and rows % rim == 0 and rows > 2 * rim:
+            return fast_shards(n, ns, snapshots, mass_blocks, neighbours, eigvecs)
+        return plain_shards(snapshots, mass_blocks, neighbours, eigvecs)
+
     in_specs = (
         P("space", "snap"),
         P(("space", "snap"), None, None, None),

time: 219 us -> 85 us (0.39)
  waiting for transfers between devices: 90.7 us -> 0 us
  Pallas kernels: 0 us -> 76.6 us
  blocking collectives: 52.9 us -> 0 us
  local copies, waits for them, and re-layouts: 36.3 us -> 6.24 us
  matrix products: 14.9 us -> 0 us
  between operations: 14.1 us -> 0.66 us
  other arithmetic: 5.77 us -> 1.3 us
  starting transfers between devices: 3.55 us -> 0 us
    pallas_call x0 -> x1, Pallas kernels: none -> 76.6 us  [fast_shards(): pl.pallas_call(functools.partial(fused, n, ns, size, 1.0 / (total * ns)),...]
    unnamed x3 -> x0, waiting for transfers between devices: 59.2 us -> none
    all_to_all x1 -> x0, blocking collectives: 52.9 us -> none  [shards(): lax.all_to_all(snapshots, 'snap', split_axis=0, concat_axis=1, tiled=True)]
    reduce_scatter x1 -> x0, waiting for transfers between devices: 31.5 us -> none  [shards(): lax.psum_scatter(partial_corr, 'snap', scatter_dimension=0, tiled=True)]
    dot_general x3 -> x0, matrix products: 14.9 us -> none  [the longest x1 7.07 us: shards(): jnp.einsum('bjrc,bjcs->brs', mass_blocks, nearby, preferred_element_type=...]
    gather x1 -> x0, local copies, waits for them, and re-layouts: 9.32 us -> none  [shards(): nearby = extended[local_ids]]
    concatenate x1 -> x0, local copies, waits for them, and re-layouts: 7.83 us -> none  [shards(): jnp.concatenate([below_rim, local_rows, above_rim], axis=0)]
    all_to_all x1 -> x0, local copies, waits for them, and re-layouts: 6.46 us -> none  [shards(): lax.all_to_all(snapshots, 'snap', split_axis=0, concat_axis=1, tiled=True)]
  transfers between devices with their start and end apart: 4 -> 0, of which waited for: 2 -> 0; matrix products, arithmetic and copies ran while one was open for 6% -> 0% of each run, Pallas kernels for 0% -> 0%
where the time goes in v2:
time: 85 us; the launch traced here: 84.8 us
  Pallas kernels  76.6 us (90%)
  local copies, waits for them, and re-layouts  6.24 us (7%)
  other arithmetic  1.3 us (2%)
    pallas_call x1, Pallas kernels, fast_shards(): pl.pallas_call(functools.partial(fused, n, ns, size, 1.0 / (total * ns)),...  76.6 us
    unnamed x7, local copies, waits for them, and re-layouts  6.15 us

profile of v2, /device:TPU:0, one launch (start us, length us, event | category | flops | bytes accessed | tf_op | source)
XLA Modules:
  0.0 84.8 jit_solution(14347045699824954383)
XLA Ops:
  0.6 0.7 subtract_add_fusion
  1.3 0.1 copy.10
  1.4 0.6 broadcast_remainder_fusion.near
  2.0 76.6 %fused.1 = (bf16[4096,512]{1,0:T(8,128)(2,1)}, bf16[4096,128]{1,0:T(8,128)(2,1)}, f32[64,128]{1,0:T(8,128)}) custom-call(s32[32,3]{1,0:T(8,128)} %broadcast_remainder_fusion.near, bf16[16384,128]{1,0:T(8,128)(2,1)} %src.1, bf16[32,3,128,128]{3,2,1,0:T(8,128)(2,1)} %mass_hbm.1, bf16[512,128]{1,0:T(8,128)(2,1)} %eig.1), custom_call_target="tpu_custom_call" | custom-call | tf_op jit(solution)/shard_map/fused/pallas_call | solution.py:268
  78.6 0.0 copy-start.1
  78.6 0.0 copy-start
  78.6 4.6 %copy.15 = bf16[4096,512]{1,0:T(8,128)(2,1)} copy(bf16[4096,512]{1,0:T(8,128)(2,1)} %get-tuple-element.12) | data formatting | bytes 8388608
  83.2 0.0 copy-done.1
  83.2 0.6 copy.16
  83.8 0.0 copy-done
  83.8 1.0 %copy.17 = bf16[4096,128]{1,0:T(8,128)(2,1)} copy(bf16[4096,128]{1,0:T(8,128)(2,1)S(1)} %copy-done) | data formatting | bytes 2097152
Async XLA Ops:
  78.6 4.6 %copy-start.1 = (f32[64,128]{1,0:T(8,128)S(1)}, f32[64,128]{1,0:T(8,128)}, u32[]{:S(2)}) copy-start(f32[64,128]{1,0:T(8,128)} %get-tuple-element.7) | copy-start | bytes 98308
  78.6 5.2 %copy-start = (bf16[4096,128]{1,0:T(8,128)(2,1)S(1)}, bf16[4096,128]{1,0:T(8,128)(2,1)}, u32[]{:S(2)}) copy-start(bf16[4096,128]{1,0:T(8,128)(2,1)} %get-tuple-element.14) | copy-start | bytes 3145732

commit v3 on v2

--- a/solution.py
+++ b/solution.py
@@ -285,9 +285,9 @@
             sem((ny, 2)), sem((ny, 2)), sem((ny, 2)), sem((ny, 2)), sem, sem, sem((nz,)), sem((nz,)),
         ],
         compiler_params=pltpu.CompilerParams(collective_id=0, has_side_effects=True,
-                                             vmem_limit_bytes=62 * 2**20),
+                                             vmem_limit_bytes=40 * 2**20),
         name="fused",
-    )(near, snapshots, mass_blocks, eigvecs)
+    )(near, pltpu.with_memory_space_constraint(snapshots, pltpu.HBM), pltpu.with_memory_space_constraint(mass_blocks, pltpu.HBM), eigvecs)
     return weighted, corr.T, modes
 
 

time: 85 us -> 82.4 us (0.969)
  local copies, waits for them, and re-layouts: 6.24 us -> 4.59 us
    unnamed x7 -> x5, local copies, waits for them, and re-layouts: 6.15 us -> 4.5 us
where the time goes in v3:
time: 82.4 us; the launch traced here: 82.2 us
  Pallas kernels  76.3 us (93%)
  local copies, waits for them, and re-layouts  4.59 us (6%)
    pallas_call x1, Pallas kernels, fast_shards(): pl.pallas_call(functools.partial(fused, n, ns, size, 1.0 / (total * ns)),...  76.3 us
    unnamed x5, local copies, waits for them, and re-layouts  4.5 us

profile of v3, /device:TPU:0, one launch (start us, length us, event | category | flops | bytes accessed | tf_op | source)
XLA Modules:
  0.0 82.2 jit_solution(14242640841470701258)
XLA Ops:
  0.6 0.7 subtract_add_fusion
  1.3 0.1 copy.10
  1.4 0.0 copy-start
  1.4 0.9 %copy-done = bf16[512,128]{1,0:T(8,128)(2,1)S(1)} copy-done((bf16[512,128]{1,0:T(8,128)(2,1)S(1)}, bf16[512,128]{1,0:T(8,128)(2,1)}, u32[]{:S(2)}) %copy-start) | copy-done | bytes 131096
  2.3 76.3 %fused.1 = (bf16[4096,512]{1,0:T(8,128)(2,1)S(1)}, bf16[4096,128]{1,0:T(8,128)(2,1)S(1)}, f32[64,128]{1,0:T(8,128)S(1)}) custom-call(s32[32,3]{1,0:T(8,128)S(1)} %broadcast_remainder_fusion.near, bf16[16384,128]{1,0:T(8,128)(2,1)} %src.1, bf16[32,3,128,128]{3,2,1,0:T(8,128)(2,1)} %mass_hbm.1, bf16[512,128]{1,0:T(8,128)(2,1)S(1)} %copy-done), custom_call_target="tpu_custom_call" | custom-call | tf_op jit(solution)/shard_map/fused/pallas_call | solution.py:268
  78.6 2.0 %copy.15 = bf16[4096,512]{1,0:T(8,128)(2,1)} copy(bf16[4096,512]{1,0:T(8,128)(2,1)S(1)} %get-tuple-element.12) | data formatting | bytes 8388608
  80.6 0.6 copy.16
  81.3 1.0 %copy.17 = bf16[4096,128]{1,0:T(8,128)(2,1)} copy(bf16[4096,128]{1,0:T(8,128)(2,1)S(1)} %get-tuple-element.14) | data formatting | bytes 2097152
  (1 shorter events, 0.0 us)
Async XLA Ops:
  1.4 0.9 %copy-start = (bf16[512,128]{1,0:T(8,128)(2,1)S(1)}, bf16[512,128]{1,0:T(8,128)(2,1)}, u32[]{:S(2)}) copy-start(bf16[512,128]{1,0:T(8,128)(2,1)} %eig.1) | copy-start | bytes 393220
